TPU v7x, 256 devices: a whole 4x4x8 slice. The times are simulated.
256 devices in a mesh: ctx: 64 (over z, y, core), hg: 4 (over x).
Axes of the slice: x: 4, y: 4, z: 8, core: 2. Of those that a mesh axis runs over, the one named last changes fastest.
Arguments:
- doc_ids: int32 [32768], P('ctx'), may hold values from 0 to 63, never falling along the last dimension, each value on 1 to 1024 neighbouring positions
- rotated_queries: bfloat16 [32768, 2048], P('ctx', 'hg'), may hold values from -6 to 6
- rotated_keys: bfloat16 [32768, 512], P('ctx', 'hg'), may hold values from -6 to 6
- value_matrix: bfloat16 [32768, 512], P('ctx', 'hg'), may hold values from -6 to 6
- out_proj: bfloat16 [4096, 2048], P('ctx', 'hg'), may hold values from -0.125 to 0.125
- cotangent: bfloat16 [32768, 4096], P('ctx'), may hold values from -16 to 16
Outputs:
- layer_output: bfloat16 [32768, 4096], P('ctx', 'hg')
- query_grad: bfloat16 [32768, 2048], P('ctx', 'hg')
- key_gradient: bfloat16 [32768, 512], P('ctx', 'hg')
- value_gradient: bfloat16 [32768, 512], P('ctx', 'hg')
- proj_grad: bfloat16 [4096, 2048], P('ctx', 'hg')
Inputs may be any that keep to these rules, and one draw needn't show every extreme that they name: `doc_ids`: document ids in token order, never falling; every document has 1 to 1024 tokens and one has exactly 1024.
All inputs are finite; a program needn't handle non-finite values.
Results may differ from a plain program's by a relative error of at most 0.013.
Values may be sent and summed in bfloat16 or wider, within the bound.
A program may use at most 128 MiB of HBM per device.

v0:
```python
import jax
import jax.numpy as jnp
from jax import lax
from jax.sharding import PartitionSpec as P

HEAD_SIZE = 128
TOK_DEV = 512
DOC_MOST = 1024


def from_behind(value, axis, by):
    devices = lax.axis_size(axis)
    pairs = [(i, i + by) for i in range(devices) if 0 <= i + by < devices]
    return lax.ppermute(value, axis, pairs)


def contract_last(left_side, right_side):
    return lax.dot_general(
        left_side, right_side, (((1,), (1,)), ((), ())), preferred_element_type=jnp.float32
    )


def contract_first(left_side, right_side):
    return lax.dot_general(
        left_side, right_side, (((0,), (0,)), ((), ())), preferred_element_type=jnp.float32
    )


def body(doc_ids, rotated_queries, rotated_keys, value_matrix, out_proj, cotangent):
    row_count = rotated_queries.shape[0]
    head_count = rotated_queries.shape[1] // HEAD_SIZE
    kv_count = rotated_keys.shape[1] // HEAD_SIZE
    group_length = head_count // kv_count
    steps_back = DOC_MOST // TOK_DEV
    score_scale = HEAD_SIZE ** (-0.5)
    device_index = lax.axis_index("ctx")
    earlier = [(rotated_keys, value_matrix, doc_ids)]
    for offset in range(1, steps_back + 1):
        earlier.append(from_behind((rotated_keys, value_matrix, doc_ids), "ctx", offset))
    ordered = earlier[::-1]
    key_cat = jnp.concatenate([member[0] for member in ordered], 0)
    value_cat = jnp.concatenate([member[1] for member in ordered], 0)
    doc_cat = jnp.concatenate([member[2] for member in ordered], 0)
    key_width = key_cat.shape[0]
    query_pos = jnp.arange(row_count, dtype=jnp.int32)
    column_pos = jnp.arange(key_width, dtype=jnp.int32)
    key_pos = column_pos - steps_back * row_count
    first_valid = (steps_back - device_index) * row_count
    allowed = (
        (doc_ids[:, None] == doc_cat[None, :])
        & (key_pos[None, :] <= query_pos[:, None])
        & (column_pos[None, :] >= first_valid)
    )
    outputs = []
    probs_list = []
    for head_index in range(head_count):
        kv_index = head_index // group_length
        query_head = rotated_queries[:, head_index * HEAD_SIZE : (head_index + 1) * HEAD_SIZE]
        key_head = key_cat
        value_head = value_cat
        scores = contract_last(query_head, key_head) * score_scale
        masked = jnp.where(allowed, scores, -jnp.inf)
        row_max = jnp.max(masked, axis=1, keepdims=True)
        row_sum = jnp.sum(jnp.where(allowed, jnp.exp(masked - row_max), 0.0), axis=1, keepdims=True)
        log_total = row_max + jnp.log(row_sum)
        weights = jnp.where(allowed, jnp.exp(masked - log_total), 0.0).astype(jnp.bfloat16)
        probs_list.append(weights)
        outputs.append(
            jnp.dot(weights, value_head, preferred_element_type=jnp.float32).astype(jnp.bfloat16)
        )
    attended = jnp.concatenate(outputs, 1)
    partial_value = contract_last(attended, lax.all_gather(out_proj, "ctx", axis=0, tiled=True))
    layer_output = lax.psum_scatter(
        partial_value.astype(jnp.bfloat16), "hg", scatter_dimension=1, tiled=True
    )
    columns = cotangent
    attention_gradient = jnp.dot(
        columns,
        lax.all_gather(out_proj, "ctx", axis=0, tiled=True),
        preferred_element_type=jnp.float32,
    ).astype(jnp.bfloat16)
    columns = cotangent
    proj_grad = lax.psum_scatter(
        contract_first(columns, attended), "ctx", scatter_dimension=0, tiled=True
    ).astype(jnp.bfloat16)
    key_parts = [jnp.zeros((key_width, HEAD_SIZE), jnp.float32)]
    value_parts = [jnp.zeros((key_width, HEAD_SIZE), jnp.float32)]
    query_grads = []
    for head_index in range(head_count):
        kv_index = head_index // group_length
        query_head = rotated_queries[:, head_index * HEAD_SIZE : (head_index + 1) * HEAD_SIZE]
        key_head = key_cat
        value_head = value_cat
        grad_head = attention_gradient[:, head_index * HEAD_SIZE : (head_index + 1) * HEAD_SIZE]
        weights = probs_list[head_index]
        row_delta = jnp.sum(
            grad_head.astype(jnp.float32) * outputs[head_index].astype(jnp.float32),
            axis=1,
            keepdims=True,
        )
        grad_dots = contract_last(grad_head, value_head)
        shifted = (weights.astype(jnp.float32) * (grad_dots - row_delta) * score_scale).astype(
            jnp.bfloat16
        )
        query_grads.append(
            jnp.dot(shifted, key_head, preferred_element_type=jnp.float32).astype(jnp.bfloat16)
        )
        key_parts[kv_index] = key_parts[kv_index] + contract_first(shifted, query_head)
        value_parts[kv_index] = value_parts[kv_index] + contract_first(weights, grad_head)
    query_grad = jnp.concatenate(query_grads, 1)
    key_all = key_parts[0]
    value_all = value_parts[0]
    pieces = []
    for offset in range(steps_back + 1):
        lower = (steps_back - offset) * row_count
        pieces.append((key_all[lower : lower + row_count], value_all[lower : lower + row_count]))
    key_sum, value_sum = pieces[0]
    for offset in range(1, steps_back + 1):
        arrived = (
            from_behind(pieces[offset][0].astype(jnp.bfloat16), "ctx", -offset).astype(jnp.float32),
            from_behind(pieces[offset][1].astype(jnp.bfloat16), "ctx", -offset).astype(jnp.float32),
        )
        key_sum = key_sum + arrived[0]
        value_sum = value_sum + arrived[1]
    key_gradient = key_sum.astype(jnp.bfloat16)
    value_gradient = value_sum.astype(jnp.bfloat16)
    return (layer_output, query_grad, key_gradient, value_gradient, proj_grad)


def solution(mesh):
    in_specs = (
        P("ctx"),
        P("ctx", "hg"),
        P("ctx", "hg"),
        P("ctx", "hg"),
        P("ctx", "hg"),
        P("ctx", None),
    )
    out_specs = (P("ctx", "hg"), P("ctx", "hg"), P("ctx", "hg"), P("ctx", "hg"), P("ctx", "hg"))
    return jax.shard_map(body, mesh=mesh, in_specs=in_specs, out_specs=out_specs, check_vma=False)
```

profile of v0, /device:TPU:1, one launch (start us, length us, event | category | flops | bytes accessed | tf_op | source)
XLA Modules:
  0.0 323.6 jit_solution(5322077553955381528)
XLA Ops:
  7.9 4.0 %collective-permute-start.2 = (bf16[512,128]{1,0:T(8,128)(2,1)}, bf16[512,128]{1,0:T(8,128)(2,1)S(1)}, u32[]{:S(2)}, u32[]{:S(2)}) collective-permute-start(bf16[512,128]{1,0:T(8,128)(2,1)} %param.8), channel_id=1, source_target_pairs={{0,8},{4,12},{8,16},{12,20},{16,24},{20,28},{24,32},{28,36},{32,40... | collective-permute-start | bytes 393224 | tf_op jit(solution)/shard_map/ppermute | solution.py:14
  12.0 4.0 %collective-permute-start.3 = (bf16[512,128]{1,0:T(8,128)(2,1)}, bf16[512,128]{1,0:T(8,128)(2,1)S(1)}, u32[]{:S(2)}, u32[]{:S(2)}) collective-permute-start(bf16[512,128]{1,0:T(8,128)(2,1)} %param.8), channel_id=1, source_target_pairs={{0,4},{4,8},{8,12},{12,16},{16,20},{20,24},{24,28},{28,32},{32,36}... | collective-permute-start | bytes 393224 | tf_op jit(solution)/shard_map/ppermute | solution.py:14
  16.0 1.9 collective-permute-start.1
  18.0 2.9 collective-permute-start
  20.9 3.2 collective-permute-start.4
  24.1 4.1 %collective-permute-start.5 = (bf16[512,128]{1,0:T(8,128)(2,1)}, bf16[512,128]{1,0:T(8,128)(2,1)S(1)}, u32[]{:S(2)}, u32[]{:S(2)}) collective-permute-start(bf16[512,128]{1,0:T(8,128)(2,1)} %param.9), channel_id=1, source_target_pairs={{0,4},{4,8},{8,12},{12,16},{16,20},{20,24},{24,28},{28,32},{32,36}... | collective-permute-start | bytes 393224 | tf_op jit(solution)/shard_map/ppermute | solution.py:14
  31.5 2.2 fusion.48
  33.8 1.2 fusion.49
  35.0 1.2 fusion.50
  36.1 1.2 fusion.51
  37.3 3.6 %select_reduce_fusion.3 = (f32[512]{0:T(512)S(1)}, f32[512]{0:T(512)S(1)}, f32[512]{0:T(512)S(1)}, f32[512]{0:T(512)S(1)}) fusion(f32[512,1536]{0,1:T(8,128)S(1)} %get-tuple-element.32, f32[512]{0:T(512)S(1)} %get-tuple-element.31, pred[1536]{0:T(1024)(128)(4,1)S(1)} %iota_compare_fusion.1, s32[1536]{0:T(1024)S(1)} %iota_add_fusion, ...), kind=kLoop, calls=%fused_computation.33 | loop fusion | flops 12580864 | bytes 12615168 | tf_op jit(solution)/shard_map/reduce_sum | solution.py:64
  40.9 4.0 %select_convert_fusion.3 = (bf16[512,1536]{0,1:T(8,128)(2,1)}, bf16[512,1536]{0,1:T(8,128)(2,1)S(1)}, bf16[512,1536]{0,1:T(8,128)(2,1)S(1)}, bf16[512,1536]{0,1:T(8,128)(2,1)S(1)}) fusion(f32[512,1536]{0,1:T(8,128)S(1)} %get-tuple-element.32, f32[512]{0:T(512)S(1)} %get-tuple-element.47, pred[1536]{0:T(1024)(128)(4,1)S(1)} %iota_compare_fusion.1, ...), kind=kLoop, calls=%fused_computation.32 | loop fusion | flops 12582912 | bytes 18898432 | tf_op jit(solution)/shard_map/convert_element_type | solution.py:66
  46.5 47.7 %all-gather.2.cloned.1.call-done = bf16[4096,512]{1,0:T(8,128)(2,1)} async-done(((bf16[64,512]{1,0:T(8,128)(2,1)}), bf16[4096,512]{1,0:T(8,128)(2,1)}) %all-gather.2.cloned.1.call-update) | async-done | bytes 4194320 | tf_op jit(solution)/shard_map/all_gather | solution.py:72
  94.2 6.0 %convolution_convert_fusion.1 = bf16[512,512]{0,1:T(8,128)(2,1)S(1)} fusion(bf16[512,4096]{1,0:T(8,128)(2,1)} %param.11, bf16[4096,512]{1,0:T(8,128)(2,1)} %all-gather.2.cloned.1.call-done), kind=kOutput, calls=%fused_computation.47 | convolution fusion | flops 2147745792 | bytes 8912896 | tf_op jit(solution)/shard_map/dot_general | solution.py:77
  102.6 5.6 %convolution_bitcast_fusion = f32[4096,512]{0,1:T(8,128)} fusion(bf16[512,4096]{1,0:T(8,128)(2,1)S(1)} %copy-done.6, bf16[512,128]{0,1:T(8,128)(2,1)S(1)} %convolution_convert_fusion.6, bf16[512,128]{0,1:T(8,128)(2,1)S(1)} %convolution_convert_fusion.7, bf16[512,128]{0,1:T(8,128)(2,1)S(1)} %convolution_convert_fusion.8, bf16[512,128]{0,1:T(8,128)(2,1)S(1)} %get-tuple-element.39), kind=kOutput, calls=%fused_computation | convolution fusion | flops 2149580800 | bytes 13107200 | tf_op jit(solution)/shard_map/dot_general | solution.py:24
  108.2 9.0 %copy.27 = f32[4096,512]{1,0:T(8,128)} copy(f32[4096,512]{0,1:T(8,128)} %convolution_bitcast_fusion) | data formatting | bytes 16777216
  117.6 6.6 %convolution_convert_fusion = bf16[512,4096]{1,0:T(8,128)(2,1)} fusion(bf16[4096,512]{1,0:T(8,128)(2,1)} %all-gather.2.cloned.1.call-done, bf16[512,128]{0,1:T(8,128)(2,1)S(1)} %convolution_convert_fusion.6, bf16[512,128]{0,1:T(8,128)(2,1)S(1)} %convolution_convert_fusion.7, bf16[512,128]{0,1:T(8,128)(2,1)S(1)} %convolution_convert_fusion.8, ...), kind=kOutput, calls=%fused_computation.1 | convolution fusion | flops 2151677952 | bytes 8912896 | tf_op jit(solution)/shard_map/dot_general | solution.py:18
  124.2 1.7 fusion.18
  126.0 1.2 copy-done.7
  128.3 1.1 copy-done.9
  131.9 1.2 copy-done.12
  134.4 2.1 copy.21
  136.4 2.2 fusion.32
  138.6 2.1 convolution_add_fusion.5
  142.0 1.3 collective-permute-start.7
  143.3 2.2 collective-permute-start.6
  147.8 1.3 collective-permute-start.9
  149.1 1.9 collective-permute-start.8
  151.8 4.2 %collective-permute-done.9 = bf16[512,128]{1,0:T(8,128)(2,1)S(1)} collective-permute-done((bf16[512,128]{1,0:T(8,128)(2,1)S(1)}, bf16[512,128]{1,0:T(8,128)(2,1)S(1)}, u32[]{:S(2)}, u32[]{:S(2)}) %collective-permute-start.9) | collective-permute-done | bytes 131104 | tf_op jit(solution)/shard_map/ppermute | solution.py:14
  155.9 1.3 collective-permute-done.8
  157.9 103.7 %reduce-scatter.7.cloned.1.call-done = f32[64,512]{1,0:T(8,128)} async-done(((f32[4096,512]{1,0:T(8,128)}), f32[64,512]{1,0:T(8,128)}) %reduce-scatter.7.cloned.1.call-update) | async-done | bytes 131088
  263.4 53.7 %reduce-scatter.5.cloned.1.call-done = bf16[512,1024]{1,0:T(8,128)(2,1)} async-done(((bf16[512,4096]{1,0:T(8,128)(2,1)}), bf16[512,1024]{1,0:T(8,128)(2,1)}) %reduce-scatter.5.cloned.1.call-update) | async-done | bytes 1048592 | tf_op jit(solution)/shard_map/reduce_scatter | solution.py:73
  (96 shorter events, 19.6 us)
Async XLA Ops:
  7.2 87.0 %all-gather.2.cloned.1.call-start = ((), (), s32[]{:S(2)}) async-start(), calls=%async_computation.2 | async-start | bytes 4259840 | tf_op jit(solution)/shard_map/all_gather | solution.py:72
  7.9 253.8 %reduce-scatter.7.cloned.1.call-start = ((), (), s32[]{:S(2)}) async-start(), calls=%async_computation.4 | async-start | bytes 8519680
  7.9 21.1 %collective-permute-start.2 = (bf16[512,128]{1,0:T(8,128)(2,1)}, bf16[512,128]{1,0:T(8,128)(2,1)S(1)}, u32[]{:S(2)}, u32[]{:S(2)}) collective-permute-start(bf16[512,128]{1,0:T(8,128)(2,1)} %param.8), channel_id=1, source_target_pairs={{0,8},{4,12},{8,16},{12,20},{16,24},{20,28},{24,32},{28,36},{32,40... | collective-permute-start | bytes 393224 | tf_op jit(solution)/shard_map/ppermute | solution.py:14
  12.0 17.0 %collective-permute-start.3 = (bf16[512,128]{1,0:T(8,128)(2,1)}, bf16[512,128]{1,0:T(8,128)(2,1)S(1)}, u32[]{:S(2)}, u32[]{:S(2)}) collective-permute-start(bf16[512,128]{1,0:T(8,128)(2,1)} %param.8), channel_id=1, source_target_pairs={{0,4},{4,8},{8,12},{12,16},{16,20},{20,24},{24,28},{28,32},{32,36}... | collective-permute-start | bytes 393224 | tf_op jit(solution)/shard_map/ppermute | solution.py:14
  16.0 8.1 %collective-permute-start.1 = (s32[512]{0:T(512)}, s32[512]{0:T(512)S(1)}, u32[]{:S(2)}, u32[]{:S(2)}) collective-permute-start(s32[512]{0:T(512)} %param.6), channel_id=1, source_target_pairs={{0,4},{4,8},{8,12},{12,16},{16,20},{20,24},{24,28},{28,32},{32,36}... | collective-permute-start | bytes 6152 | tf_op jit(solution)/shard_map/ppermute | solution.py:14
  18.0 10.3 %collective-permute-start = (s32[512]{0:T(512)}, s32[512]{0:T(512)S(1)}, u32[]{:S(2)}, u32[]{:S(2)}) collective-permute-start(s32[512]{0:T(512)} %param.6), channel_id=1, source_target_pairs={{0,8},{4,12},{8,16},{12,20},{16,24},{20,28},{24,32},{28,36},{32,40... | collective-permute-start | bytes 6152 | tf_op jit(solution)/shard_map/ppermute | solution.py:14
  20.9 9.1 %collective-permute-start.4 = (bf16[512,128]{1,0:T(8,128)(2,1)}, bf16[512,128]{1,0:T(8,128)(2,1)S(1)}, u32[]{:S(2)}, u32[]{:S(2)}) collective-permute-start(bf16[512,128]{1,0:T(8,128)(2,1)} %param.9), channel_id=1, source_target_pairs={{0,8},{4,12},{8,16},{12,20},{16,24},{20,28},{24,32},{28,36},{32,40... | collective-permute-start | bytes 393224 | tf_op jit(solution)/shard_map/ppermute | solution.py:14
  24.1 6.4 %collective-permute-start.5 = (bf16[512,128]{1,0:T(8,128)(2,1)}, bf16[512,128]{1,0:T(8,128)(2,1)S(1)}, u32[]{:S(2)}, u32[]{:S(2)}) collective-permute-start(bf16[512,128]{1,0:T(8,128)(2,1)} %param.9), channel_id=1, source_target_pairs={{0,4},{4,8},{8,12},{12,16},{16,20},{20,24},{24,28},{28,32},{32,36}... | collective-permute-start | bytes 393224 | tf_op jit(solution)/shard_map/ppermute | solution.py:14
  30.0 6.2 %copy-start.19 = (bf16[1536,128]{1,0:T(8,128)(2,1)}, bf16[1536,128]{1,0:T(8,128)(2,1)S(1)}, u32[]{:S(2)}) copy-start(bf16[1536,128]{1,0:T(8,128)(2,1)S(1)} %constant_dynamic-update-slice_fusion) | copy-start | bytes 1179652
  31.5 14.3 %copy-start.21 = (bf16[1536,128]{1,0:T(8,128)(2,1)}, bf16[1536,128]{1,0:T(8,128)(2,1)S(1)}, u32[]{:S(2)}) copy-start(bf16[1536,128]{1,0:T(8,128)(2,1)S(1)} %constant_dynamic-update-slice_fusion.3) | copy-start | bytes 1179652
  31.5 2.3 copy-start.13
  31.5 2.3 copy-start.24
  94.2 6.0 %copy-start.3 = (bf16[512,1536]{0,1:T(8,128)(2,1)S(1)}, bf16[512,1536]{0,1:T(8,128)(2,1)}, u32[]{:S(2)}) copy-start(bf16[512,1536]{0,1:T(8,128)(2,1)} %get-tuple-element.27) | copy-start | bytes 4718596
  94.2 6.0 %copy-start.22 = (bf16[1536,128]{1,0:T(8,128)(2,1)S(1)}, bf16[1536,128]{1,0:T(8,128)(2,1)}, u32[]{:S(2)}) copy-start(bf16[1536,128]{1,0:T(8,128)(2,1)} %copy-done.21) | copy-start | bytes 1179652
  100.2 2.4 copy-start.6
  117.3 199.8 %reduce-scatter.5.cloned.1.call-start = ((), (), s32[]{:S(2)}) async-start(), calls=%async_computation.3 | async-start | bytes 5242880 | tf_op jit(solution)/shard_map/reduce_scatter | solution.py:73
  124.2 3.0 copy-start.20
  124.2 3.4 %copy-start.16 = (bf16[512,512]{0,1:T(8,128)(2,1)S(1)}, bf16[512,512]{0,1:T(8,128)(2,1)}, u32[]{:S(2)}) copy-start(bf16[512,512]{0,1:T(8,128)(2,1)} %copy-done.15) | copy-start | bytes 1572868
  124.2 3.4 %copy-start.23 = (bf16[1536,128]{1,0:T(8,128)(2,1)S(1)}, bf16[1536,128]{1,0:T(8,128)(2,1)}, u32[]{:S(2)}) copy-start(bf16[1536,128]{1,0:T(8,128)(2,1)} %copy-done.21) | copy-start | bytes 1179652
  127.6 2.2 copy-start.1
  129.8 1.5 copy-start.4
  130.5 3.0 copy-start.11
  136.4 4.3 %copy-start.10 = (bf16[512,1536]{0,1:T(8,128)(2,1)S(1)}, bf16[512,1536]{0,1:T(8,128)(2,1)}, u32[]{:S(2)}) copy-start(bf16[512,1536]{0,1:T(8,128)(2,1)} %copy-done.9) | copy-start | bytes 4718596
  136.4 4.3 %copy-start.14 = (bf16[512,512]{1,0:T(8,128)(2,1)S(1)}, bf16[512,512]{1,0:T(8,128)(2,1)}, u32[]{:S(2)}) copy-start(bf16[512,512]{1,0:T(8,128)(2,1)} %param.7) | copy-start | bytes 1572868
  138.6 2.8 copy-start.8
  140.8 4.7 %copy-start.5 = (bf16[512,1536]{0,1:T(8,128)(2,1)S(1)}, bf16[512,1536]{0,1:T(8,128)(2,1)}, u32[]{:S(2)}) copy-start(bf16[512,1536]{0,1:T(8,128)(2,1)} %get-tuple-element.27) | copy-start | bytes 4718596
  140.8 4.7 %copy-start.17 = (bf16[512,512]{0,1:T(8,128)(2,1)S(1)}, bf16[512,512]{0,1:T(8,128)(2,1)}, u32[]{:S(2)}) copy-start(bf16[512,512]{0,1:T(8,128)(2,1)} %copy-done.15) | copy-start | bytes 1572868
  141.4 4.7 %copy-start.2 = (bf16[512,1536]{0,1:T(8,128)(2,1)S(1)}, bf16[512,1536]{0,1:T(8,128)(2,1)}, u32[]{:S(2)}) copy-start(bf16[512,1536]{0,1:T(8,128)(2,1)} %copy-done) | copy-start | bytes 4718596
  142.0 9.0 %collective-permute-start.7 = (bf16[512,128]{1,0:T(8,128)(2,1)S(1)}, bf16[512,128]{1,0:T(8,128)(2,1)S(1)}, u32[]{:S(2)}, u32[]{:S(2)}) collective-permute-start(bf16[512,128]{1,0:T(8,128)(2,1)S(1)} %get-tuple-element.26), channel_id=1, source_target_pairs={{8,0},{12,4},{16,8},{20,12},{24,16},{28,20},{32,24},{36,28},{40,32... | collective-permute-start | bytes 393224 | tf_op jit(solution)/shard_map/ppermute | solution.py:14
  143.3 7.8 %collective-permute-start.6 = (bf16[512,128]{1,0:T(8,128)(2,1)S(1)}, bf16[512,128]{1,0:T(8,128)(2,1)S(1)}, u32[]{:S(2)}, u32[]{:S(2)}) collective-permute-start(bf16[512,128]{1,0:T(8,128)(2,1)S(1)} %get-tuple-element.25), channel_id=1, source_target_pairs={{4,0},{8,4},{12,8},{16,12},{20,16},{24,20},{28,24},{32,28},{36,32}... | collective-permute-start | bytes 393224 | tf_op jit(solution)/shard_map/ppermute | solution.py:14
  147.8 8.1 %collective-permute-start.9 = (bf16[512,128]{1,0:T(8,128)(2,1)S(1)}, bf16[512,128]{1,0:T(8,128)(2,1)S(1)}, u32[]{:S(2)}, u32[]{:S(2)}) collective-permute-start(bf16[512,128]{1,0:T(8,128)(2,1)S(1)} %get-tuple-element.24), channel_id=1, source_target_pairs={{8,0},{12,4},{16,8},{20,12},{24,16},{28,20},{32,24},{36,28},{40,32... | collective-permute-start | bytes 393224 | tf_op jit(solution)/shard_map/ppermute | solution.py:14
  149.1 8.1 %collective-permute-start.8 = (bf16[512,128]{1,0:T(8,128)(2,1)S(1)}, bf16[512,128]{1,0:T(8,128)(2,1)S(1)}, u32[]{:S(2)}, u32[]{:S(2)}) collective-permute-start(bf16[512,128]{1,0:T(8,128)(2,1)S(1)} %get-tuple-element.23), channel_id=1, source_target_pairs={{4,0},{8,4},{12,8},{16,12},{20,16},{24,20},{28,24},{32,28},{36,32}... | collective-permute-start | bytes 393224 | tf_op jit(solution)/shard_map/ppermute | solution.py:14
  (6 other events, 6.1 us)
Sparse Core Ops, SparseCore 0:
  10.7 83.4 all-gather.1
  117.4 144.2 reduce-scatter.6
  264.8 52.2 reduce-scatter.4
where the time goes:
time: 324 us
  waiting for transfers between devices  212 us (65%)
  matrix products  38.7 us (12%)
  starting transfers between devices  27.3 us (8%)
  local copies, waits for them, and re-layouts  20.9 us (6%)
  between operations  14.4 us (4%)
  other arithmetic  10.5 us (3%)
    unnamed x4, waiting for transfers between devices  104 us
    reduce_scatter x1, waiting for transfers between devices, body(): lax.psum_scatter(partial_value.astype(jnp.bfloat16), 'hg', scatter_dimens...  53.7 us
    all_gather x1, waiting for transfers between devices, body(): lax.all_gather(out_proj, 'ctx', axis=0, tiled=True)  47.7 us
    ppermute x10, starting transfers between devices, from_behind(): return lax.ppermute(value, axis, pairs)  26.9 us
    unnamed x58, local copies, waits for them, and re-layouts  19 us
    dot_general x9, matrix products, contract_last(): lax.dot_general(left_side, right_side, (((1,), (1,)), ((), ())), preferre...  16 us
    dot_general x9, matrix products, contract_first(): lax.dot_general(left_side, right_side, (((0,), (0,)), ((), ())), preferre...  13.3 us
  transfers between devices with their start and end apart: 13, of which 6 were waited for; matrix products, arithmetic and copies ran while one was open for 13% of the time, Pallas kernels for 0%

commit v1 on v0

--- a/solution.py
+++ b/solution.py
@@ -69,7 +69,12 @@
             jnp.dot(weights, value_head, preferred_element_type=jnp.float32).astype(jnp.bfloat16)
         )
     attended = jnp.concatenate(outputs, 1)
-    partial_value = contract_last(attended, lax.all_gather(out_proj, "ctx", axis=0, tiled=True))
+    partial_value = contract_last(
+        attended,
+        jnp.concatenate(
+            lax.all_to_all(jnp.stack([out_proj] * lax.axis_size("ctx")), "ctx", 0, 0), axis=0
+        ),
+    )
     layer_output = lax.psum_scatter(
         partial_value.astype(jnp.bfloat16), "hg", scatter_dimension=1, tiled=True
     )

time: 324 us -> 339 us (1.046)
  blocking collectives: 0 us -> 109 us
  waiting for transfers between devices: 212 us -> 114 us
    all_to_all x0 -> x1, blocking collectives: none -> 109 us  [body(): lax.all_to_all(jnp.stack([out_proj] * lax.axis_size('ctx')), 'ctx', 0, 0)]
    unnamed x4, waiting for transfers between devices: 104 us -> 6.17 us
    unnamed x58 -> x68, local copies, waits for them, and re-layouts: 19 us -> 21.4 us
  transfers between devices with their start and end apart: 13 -> 13, of which waited for: 6 -> 7; matrix products, arithmetic and copies ran while one was open for 13% -> 12% of each run, Pallas kernels for 0% -> 0%
where the time goes in v1:
time: 339 us; the launch traced here: 338 us
  waiting for transfers between devices  114 us (34%)
  blocking collectives  109 us (32%)
  matrix products  36.2 us (11%)
  starting transfers between devices  29.5 us (9%)
  local copies, waits for them, and re-layouts  23.9 us (7%)
  between operations  14.4 us (4%)
  other arithmetic  10.5 us (3%)
    all_to_all x1, blocking collectives, body(): lax.all_to_all(jnp.stack([out_proj] * lax.axis_size('ctx')), 'ctx', 0, 0)  109 us
    reduce_scatter x1, waiting for transfers between devices, body(): lax.psum_scatter(partial_value.astype(jnp.bfloat16), 'hg', scatter_dimens...  53.3 us
    all_gather x1, waiting for transfers between devices, body(): lax.all_gather(out_proj, 'ctx', axis=0, tiled=True)  45.3 us
    ppermute x10, starting transfers between devices, from_behind(): return lax.ppermute(value, axis, pairs)  29.4 us
    unnamed x68, local copies, waits for them, and re-layouts  21.4 us
    dot_general x9, matrix products, contract_last(): lax.dot_general(left_side, right_side, (((1,), (1,)), ((), ())), preferre...  13.5 us
    dot_general x9, matrix products, contract_first(): lax.dot_general(left_side, right_side, (((0,), (0,)), ((), ())), preferre...  12.6 us
    ppermute x10, waiting for transfers between devices, from_behind(): return lax.ppermute(value, axis, pairs)  9.06 us
  transfers between devices with their start and end apart: 13, of which 7 were waited for; matrix products, arithmetic and copies ran while one was open for 12% of the time, Pallas kernels for 0%

profile of v1, /device:TPU:1, one launch (start us, length us, event | category | flops | bytes accessed | tf_op | source)
XLA Modules:
  0.0 337.7 jit_solution(4651847398898579982)
XLA Ops:
  7.9 4.0 %collective-permute-start = (s32[512]{0:T(512)}, s32[512]{0:T(512)S(1)}, u32[]{:S(2)}, u32[]{:S(2)}) collective-permute-start(s32[512]{0:T(512)} %param.6), channel_id=1, source_target_pairs={{0,8},{4,12},{8,16},{12,20},{16,24},{20,28},{24,32},{28,36},{32,40... | collective-permute-start | bytes 6152 | tf_op jit(solution)/shard_map/ppermute | solution.py:14
  12.0 4.1 %collective-permute-start.1 = (s32[512]{0:T(512)}, s32[512]{0:T(512)S(1)}, u32[]{:S(2)}, u32[]{:S(2)}) collective-permute-start(s32[512]{0:T(512)} %param.6), channel_id=1, source_target_pairs={{0,4},{4,8},{8,12},{12,16},{16,20},{20,24},{24,28},{28,32},{32,36}... | collective-permute-start | bytes 6152 | tf_op jit(solution)/shard_map/ppermute | solution.py:14
  16.0 2.9 collective-permute-start.2
  19.0 2.2 collective-permute-start.3
  21.2 3.2 collective-permute-start.4
  24.4 3.6 %collective-permute-start.5 = (bf16[512,128]{1,0:T(8,128)(2,1)}, bf16[512,128]{1,0:T(8,128)(2,1)S(1)}, u32[]{:S(2)}, u32[]{:S(2)}) collective-permute-start(bf16[512,128]{1,0:T(8,128)(2,1)} %param.9), channel_id=1, source_target_pairs={{0,4},{4,8},{8,12},{12,16},{16,20},{20,24},{24,28},{28,32},{32,36}... | collective-permute-start | bytes 393224 | tf_op jit(solution)/shard_map/ppermute | solution.py:14
  28.7 1.6 collective-permute-done.5
  32.4 2.2 fusion.51
  34.7 1.2 fusion.50
  35.9 1.2 fusion.49
  37.1 1.2 fusion.48
  38.2 3.6 %select_reduce_fusion.3 = (f32[512]{0:T(512)S(1)}, f32[512]{0:T(512)S(1)}, f32[512]{0:T(512)S(1)}, f32[512]{0:T(512)S(1)}) fusion(f32[512,1536]{0,1:T(8,128)S(1)} %get-tuple-element.32, f32[512]{0:T(512)S(1)} %get-tuple-element.31, pred[1536]{0:T(1024)(128)(4,1)S(1)} %iota_compare_fusion.1, s32[1536]{0:T(1024)S(1)} %iota_add_fusion, ...), kind=kLoop, calls=%fused_computation.33 | loop fusion | flops 12580864 | bytes 12615168 | tf_op jit(solution)/shard_map/reduce_sum | solution.py:64
  41.8 4.0 %select_convert_fusion.3 = (bf16[512,1536]{0,1:T(8,128)(2,1)}, bf16[512,1536]{0,1:T(8,128)(2,1)S(1)}, bf16[512,1536]{0,1:T(8,128)(2,1)S(1)}, bf16[512,1536]{0,1:T(8,128)(2,1)S(1)}) fusion(f32[512,1536]{0,1:T(8,128)S(1)} %get-tuple-element.32, f32[512]{0:T(512)S(1)} %get-tuple-element.47, pred[1536]{0:T(1024)(128)(4,1)S(1)} %iota_compare_fusion.1, ...), kind=kLoop, calls=%fused_computation.32 | loop fusion | flops 12582912 | bytes 18898432 | tf_op jit(solution)/shard_map/convert_element_type | solution.py:66
  48.9 45.3 %all-gather.2.cloned.1.call-done = bf16[4096,512]{1,0:T(8,128)(2,1)} async-done(((bf16[64,512]{1,0:T(8,128)(2,1)}), bf16[4096,512]{1,0:T(8,128)(2,1)}) %all-gather.2.cloned.1.call-update) | async-done | bytes 4194320 | tf_op jit(solution)/shard_map/all_gather | solution.py:84
  94.2 6.0 %convolution_convert_fusion.1 = bf16[512,512]{0,1:T(8,128)(2,1)S(1)} fusion(bf16[512,4096]{1,0:T(8,128)(2,1)} %param.11, bf16[4096,512]{1,0:T(8,128)(2,1)} %all-gather.2.cloned.1.call-done), kind=kOutput, calls=%fused_computation.47 | convolution fusion | flops 2147745792 | bytes 8912896 | tf_op jit(solution)/shard_map/dot_general | solution.py:82
  102.6 5.6 %convolution_bitcast_fusion = f32[4096,512]{0,1:T(8,128)} fusion(bf16[512,4096]{1,0:T(8,128)(2,1)S(1)} %copy-done.5, bf16[512,128]{0,1:T(8,128)(2,1)S(1)} %copy-done.20, bf16[512,128]{0,1:T(8,128)(2,1)S(1)} %convolution_convert_fusion.7, bf16[512,128]{0,1:T(8,128)(2,1)S(1)} %convolution_convert_fusion.8, bf16[512,128]{0,1:T(8,128)(2,1)S(1)} %get-tuple-element.39), kind=kOutput, calls=%fused_computation | convolution fusion | flops 2149580800 | bytes 13107200 | tf_op jit(solution)/shard_map/dot_general | solution.py:24
  108.2 9.0 %copy.27 = f32[4096,512]{1,0:T(8,128)} copy(f32[4096,512]{0,1:T(8,128)} %convolution_bitcast_fusion) | data formatting | bytes 16777216
  118.6 109.5 %all_to_all.5 = bf16[64,64,512]{2,1,0:T(8,128)(2,1)S(1)} all-to-all(bf16[64,64,512]{2,1,0:T(8,128)(2,1)S(1)} %stack.2), channel_id=1, replica_groups=mesh['ctx'=64,'hg'=4] {'ctx'}, dimensions={0} | all-to-all | bytes 8388608 | tf_op jit(solution)/shard_map/all_to_all | solution.py:75
  228.1 4.4 %convolution_convert_fusion = bf16[512,4096]{1,0:T(8,128)(2,1)} fusion(bf16[4096,512]{1,0:T(8,128)(2,1)S(1)} %bitcast.56, bf16[512,128]{0,1:T(8,128)(2,1)S(1)} %copy-done.21, bf16[512,128]{0,1:T(8,128)(2,1)S(1)} %convolution_convert_fusion.7, bf16[512,128]{0,1:T(8,128)(2,1)S(1)} %convolution_convert_fusion.8, bf16[512,128]{0,1:T(8,128)(2,1)S(1)} %copy-done.23), kind=kOutput, calls=%fused_computation.1 | convolution fusion | flops 2151677952 | bytes 8912896 | tf_op jit(solution)/shard_map/dot_general | solution.py:18
  233.5 1.5 fusion.19
  242.9 2.0 copy.21
  244.9 2.1 fusion.41
  247.1 1.5 convolution_add_fusion.2
  249.8 4.9 %collective-permute-start.8 = (bf16[512,128]{1,0:T(8,128)(2,1)S(1)}, bf16[512,128]{1,0:T(8,128)(2,1)S(1)}, u32[]{:S(2)}, u32[]{:S(2)}) collective-permute-start(bf16[512,128]{1,0:T(8,128)(2,1)S(1)} %get-tuple-element.23), channel_id=1, source_target_pairs={{4,0},{8,4},{12,8},{16,12},{20,16},{24,20},{28,24},{32,28},{36,32}... | collective-permute-start | bytes 393224 | tf_op jit(solution)/shard_map/ppermute | solution.py:14
  254.7 1.3 collective-permute-start.9
  258.6 1.9 collective-permute-start.6
  260.5 1.3 collective-permute-start.7
  261.8 1.6 collective-permute-done.9
  264.2 2.1 collective-permute-done.6
  266.3 3.7 %collective-permute-done.7 = bf16[512,128]{1,0:T(8,128)(2,1)S(1)} collective-permute-done((bf16[512,128]{1,0:T(8,128)(2,1)S(1)}, bf16[512,128]{1,0:T(8,128)(2,1)S(1)}, u32[]{:S(2)}, u32[]{:S(2)}) %collective-permute-start.7) | collective-permute-done | bytes 131104 | tf_op jit(solution)/shard_map/ppermute | solution.py:14
  270.7 5.5 %reduce-scatter.7.cloned.1.call-done = f32[64,512]{1,0:T(8,128)} async-done(((f32[4096,512]{1,0:T(8,128)}), f32[64,512]{1,0:T(8,128)}) %reduce-scatter.7.cloned.1.call-update) | async-done | bytes 131088
  277.9 53.3 %reduce-scatter.5.cloned.1.call-done = bf16[512,1024]{1,0:T(8,128)(2,1)} async-done(((bf16[512,4096]{1,0:T(8,128)(2,1)}), bf16[512,1024]{1,0:T(8,128)(2,1)}) %reduce-scatter.5.cloned.1.call-update) | async-done | bytes 1048592 | tf_op jit(solution)/shard_map/reduce_scatter | solution.py:78
  (108 shorter events, 25.9 us)
Async XLA Ops:
  7.2 87.0 %all-gather.2.cloned.1.call-start = ((), (), s32[]{:S(2)}) async-start(), calls=%async_computation.4 | async-start | bytes 4259840 | tf_op jit(solution)/shard_map/all_gather | solution.py:84
  7.9 268.2 %reduce-scatter.7.cloned.1.call-start = ((), (), s32[]{:S(2)}) async-start(), calls=%async_computation.5 | async-start | bytes 8519680
  7.9 16.5 %collective-permute-start = (s32[512]{0:T(512)}, s32[512]{0:T(512)S(1)}, u32[]{:S(2)}, u32[]{:S(2)}) collective-permute-start(s32[512]{0:T(512)} %param.6), channel_id=1, source_target_pairs={{0,8},{4,12},{8,16},{12,20},{16,24},{20,28},{24,32},{28,36},{32,40... | collective-permute-start | bytes 6152 | tf_op jit(solution)/shard_map/ppermute | solution.py:14
  12.0 16.1 %collective-permute-start.1 = (s32[512]{0:T(512)}, s32[512]{0:T(512)S(1)}, u32[]{:S(2)}, u32[]{:S(2)}) collective-permute-start(s32[512]{0:T(512)} %param.6), channel_id=1, source_target_pairs={{0,4},{4,8},{8,12},{12,16},{16,20},{20,24},{24,28},{28,32},{32,36}... | collective-permute-start | bytes 6152 | tf_op jit(solution)/shard_map/ppermute | solution.py:14
  16.0 15.3 %collective-permute-start.2 = (bf16[512,128]{1,0:T(8,128)(2,1)}, bf16[512,128]{1,0:T(8,128)(2,1)S(1)}, u32[]{:S(2)}, u32[]{:S(2)}) collective-permute-start(bf16[512,128]{1,0:T(8,128)(2,1)} %param.8), channel_id=1, source_target_pairs={{0,8},{4,12},{8,16},{12,20},{16,24},{20,28},{24,32},{28,36},{32,40... | collective-permute-start | bytes 393224 | tf_op jit(solution)/shard_map/ppermute | solution.py:14
  19.0 12.4 %collective-permute-start.3 = (bf16[512,128]{1,0:T(8,128)(2,1)}, bf16[512,128]{1,0:T(8,128)(2,1)S(1)}, u32[]{:S(2)}, u32[]{:S(2)}) collective-permute-start(bf16[512,128]{1,0:T(8,128)(2,1)} %param.8), channel_id=1, source_target_pairs={{0,4},{4,8},{8,12},{12,16},{16,20},{20,24},{24,28},{28,32},{32,36}... | collective-permute-start | bytes 393224 | tf_op jit(solution)/shard_map/ppermute | solution.py:14
  21.2 7.6 %collective-permute-start.4 = (bf16[512,128]{1,0:T(8,128)(2,1)}, bf16[512,128]{1,0:T(8,128)(2,1)S(1)}, u32[]{:S(2)}, u32[]{:S(2)}) collective-permute-start(bf16[512,128]{1,0:T(8,128)(2,1)} %param.9), channel_id=1, source_target_pairs={{0,8},{4,12},{8,16},{12,20},{16,24},{20,28},{24,32},{28,36},{32,40... | collective-permute-start | bytes 393224 | tf_op jit(solution)/shard_map/ppermute | solution.py:14
  24.4 5.9 %collective-permute-start.5 = (bf16[512,128]{1,0:T(8,128)(2,1)}, bf16[512,128]{1,0:T(8,128)(2,1)S(1)}, u32[]{:S(2)}, u32[]{:S(2)}) collective-permute-start(bf16[512,128]{1,0:T(8,128)(2,1)} %param.9), channel_id=1, source_target_pairs={{0,4},{4,8},{8,12},{12,16},{16,20},{20,24},{24,28},{28,32},{32,36}... | collective-permute-start | bytes 393224 | tf_op jit(solution)/shard_map/ppermute | solution.py:14
  31.3 16.5 %copy-start.24 = (bf16[1536,128]{1,0:T(8,128)(2,1)}, bf16[1536,128]{1,0:T(8,128)(2,1)S(1)}, u32[]{:S(2)}) copy-start(bf16[1536,128]{1,0:T(8,128)(2,1)S(1)} %constant_dynamic-update-slice_fusion.3) | copy-start | bytes 1179652
  32.4 4.7 %copy-start.27 = (bf16[1536,128]{1,0:T(8,128)(2,1)}, bf16[1536,128]{1,0:T(8,128)(2,1)S(1)}, u32[]{:S(2)}) copy-start(bf16[1536,128]{1,0:T(8,128)(2,1)S(1)} %constant_dynamic-update-slice_fusion) | copy-start | bytes 1179652
  32.4 2.3 copy-start.14
  32.4 2.3 copy-start.29
  94.2 6.0 %copy-start.3 = (bf16[512,1536]{0,1:T(8,128)(2,1)S(1)}, bf16[512,1536]{0,1:T(8,128)(2,1)}, u32[]{:S(2)}) copy-start(bf16[512,1536]{0,1:T(8,128)(2,1)} %get-tuple-element.27) | copy-start | bytes 4718596
  94.2 6.0 %copy-start.20 = (bf16[512,128]{0,1:T(8,128)(2,1)S(1)}, bf16[512,128]{0,1:T(8,128)(2,1)}, u32[]{:S(2)}) copy-start(bf16[512,128]{0,1:T(8,128)(2,1)} %convolution_convert_fusion.6) | copy-start | bytes 393220
  94.2 6.0 %copy-start.25 = (bf16[1536,128]{1,0:T(8,128)(2,1)S(1)}, bf16[1536,128]{1,0:T(8,128)(2,1)}, u32[]{:S(2)}) copy-start(bf16[1536,128]{1,0:T(8,128)(2,1)} %copy-done.24) | copy-start | bytes 1179652
  100.2 2.4 copy-start.5
  117.3 213.9 %reduce-scatter.5.cloned.1.call-start = ((), (), s32[]{:S(2)}) async-start(), calls=%async_computation.3 | async-start | bytes 5242880 | tf_op jit(solution)/shard_map/reduce_scatter | solution.py:78
  118.6 109.5 %copy-start.21 = (bf16[512,128]{0,1:T(8,128)(2,1)S(1)}, bf16[512,128]{0,1:T(8,128)(2,1)}, u32[]{:S(2)}) copy-start(bf16[512,128]{0,1:T(8,128)(2,1)} %convolution_convert_fusion.6) | copy-start | bytes 393220
  118.6 109.5 %copy-start.23 = (bf16[512,128]{0,1:T(8,128)(2,1)S(1)}, bf16[512,128]{0,1:T(8,128)(2,1)}, u32[]{:S(2)}) copy-start(bf16[512,128]{0,1:T(8,128)(2,1)} %copy-done.22) | copy-start | bytes 393220
  232.5 3.7 %copy-start.28 = (bf16[1536,128]{1,0:T(8,128)(2,1)S(1)}, bf16[1536,128]{1,0:T(8,128)(2,1)}, u32[]{:S(2)}) copy-start(bf16[1536,128]{1,0:T(8,128)(2,1)} %copy-done.27) | copy-start | bytes 1179652
  232.5 4.1 %copy-start.1 = (bf16[512,1536]{0,1:T(8,128)(2,1)S(1)}, bf16[512,1536]{0,1:T(8,128)(2,1)}, u32[]{:S(2)}) copy-start(bf16[512,1536]{0,1:T(8,128)(2,1)} %copy-done) | copy-start | bytes 4718596
  232.5 4.1 %copy-start.17 = (bf16[512,512]{0,1:T(8,128)(2,1)S(1)}, bf16[512,512]{0,1:T(8,128)(2,1)}, u32[]{:S(2)}) copy-start(bf16[512,512]{0,1:T(8,128)(2,1)} %copy-done.16) | copy-start | bytes 1572868
  244.9 2.1 copy-start.2
  244.9 3.6 %copy-start.18 = (bf16[512,512]{0,1:T(8,128)(2,1)S(1)}, bf16[512,512]{0,1:T(8,128)(2,1)}, u32[]{:S(2)}) copy-start(bf16[512,512]{0,1:T(8,128)(2,1)} %copy-done.16) | copy-start | bytes 1572868
  248.6 7.4 %copy-start.13 = (bf16[512,1536]{0,1:T(8,128)(2,1)S(1)}, bf16[512,1536]{0,1:T(8,128)(2,1)}, u32[]{:S(2)}) copy-start(bf16[512,1536]{0,1:T(8,128)(2,1)} %copy-done.12) | copy-start | bytes 4718596
  248.6 7.4 %copy-start.15 = (bf16[512,512]{1,0:T(8,128)(2,1)S(1)}, bf16[512,512]{1,0:T(8,128)(2,1)}, u32[]{:S(2)}) copy-start(bf16[512,512]{1,0:T(8,128)(2,1)} %param.7) | copy-start | bytes 1572868
  249.2 7.4 %copy-start.11 = (bf16[512,1536]{0,1:T(8,128)(2,1)S(1)}, bf16[512,1536]{0,1:T(8,128)(2,1)}, u32[]{:S(2)}) copy-start(bf16[512,1536]{0,1:T(8,128)(2,1)} %copy-done.10) | copy-start | bytes 4718596
  249.8 7.4 %copy-start.9 = (bf16[512,1536]{0,1:T(8,128)(2,1)S(1)}, bf16[512,1536]{0,1:T(8,128)(2,1)}, u32[]{:S(2)}) copy-start(bf16[512,1536]{0,1:T(8,128)(2,1)} %copy-done.8) | copy-start | bytes 4718596
  249.8 12.0 %collective-permute-start.8 = (bf16[512,128]{1,0:T(8,128)(2,1)S(1)}, bf16[512,128]{1,0:T(8,128)(2,1)S(1)}, u32[]{:S(2)}, u32[]{:S(2)}) collective-permute-start(bf16[512,128]{1,0:T(8,128)(2,1)S(1)} %get-tuple-element.23), channel_id=1, source_target_pairs={{4,0},{8,4},{12,8},{16,12},{20,16},{24,20},{28,24},{32,28},{36,32}... | collective-permute-start | bytes 393224 | tf_op jit(solution)/shard_map/ppermute | solution.py:14
  254.7 8.8 %collective-permute-start.9 = (bf16[512,128]{1,0:T(8,128)(2,1)S(1)}, bf16[512,128]{1,0:T(8,128)(2,1)S(1)}, u32[]{:S(2)}, u32[]{:S(2)}) collective-permute-start(bf16[512,128]{1,0:T(8,128)(2,1)S(1)} %get-tuple-element.24), channel_id=1, source_target_pairs={{8,0},{12,4},{16,8},{20,12},{24,16},{28,20},{32,24},{36,28},{40,32... | collective-permute-start | bytes 393224 | tf_op jit(solution)/shard_map/ppermute | solution.py:14
  258.6 7.7 %collective-permute-start.6 = (bf16[512,128]{1,0:T(8,128)(2,1)S(1)}, bf16[512,128]{1,0:T(8,128)(2,1)S(1)}, u32[]{:S(2)}, u32[]{:S(2)}) collective-permute-start(bf16[512,128]{1,0:T(8,128)(2,1)S(1)} %get-tuple-element.25), channel_id=1, source_target_pairs={{4,0},{8,4},{12,8},{16,12},{20,16},{24,20},{28,24},{32,28},{36,32}... | collective-permute-start | bytes 393224 | tf_op jit(solution)/shard_map/ppermute | solution.py:14
  260.5 9.4 %collective-permute-start.7 = (bf16[512,128]{1,0:T(8,128)(2,1)S(1)}, bf16[512,128]{1,0:T(8,128)(2,1)S(1)}, u32[]{:S(2)}, u32[]{:S(2)}) collective-permute-start(bf16[512,128]{1,0:T(8,128)(2,1)S(1)} %get-tuple-element.26), channel_id=1, source_target_pairs={{8,0},{12,4},{16,8},{20,12},{24,16},{28,20},{32,24},{36,28},{40,32... | collective-permute-start | bytes 393224 | tf_op jit(solution)/shard_map/ppermute | solution.py:14
  (11 other events, 12.7 us)
Sparse Core Ops, SparseCore 0:
  10.7 83.3 all-gather.1
  117.4 158.6 reduce-scatter.6
  279.3 51.8 reduce-scatter.4
